TPU v7x, 512 devices: a whole 4x8x8 slice. The times are simulated.
512 devices in a mesh: blk: 16 (over z_lo, x), lab: 32 (over y, z_hi, core).
Axes of the slice: x: 4, y: 8, z: 8 (z_hi: 2, z_lo: 4; z = z_hi * 4 + z_lo), core: 2. Of those that a mesh axis runs over, the one named last changes fastest.
Arguments:
- features: bfloat16 [65536, 768], P(('blk', 'lab')), may hold values from -0.21875 to 0.21875
- direction: bfloat16 [32, 256, 768], P('lab', 'blk'), may hold values from -6 to 6
- active: int32 [65536, 8192], P('blk', 'lab'), may hold values 0 or 1
- shortlist: int32 [512, 64], P('blk', 'lab'), may hold values 0 or 1
Outputs:
- hess_product: float32 [32, 256, 768], P('lab', 'blk')
- curvature: float32 [32, 256], P('lab', 'blk')
All inputs are finite; a program needn't handle non-finite values. No bound on the sum of `active` or of `shortlist` on one device may be relied on, other than what follows from the above.
Results may differ from a plain program's by a relative error of at most 0.00059.
Values may be sent and summed in bfloat16 or wider, within the bound.
No kernel may reach another device: no remote copies, remote signals or barrier semaphores. Data moves between devices by JAX's collectives and lax.ppermute only.
A program may use at most 64 MiB of HBM per device.

v0:
```python
import jax
import jax.numpy as jnp
from jax import lax
from jax.sharding import PartitionSpec as P

D = 768
TILE = 128


def active_weights(active, shortlist):
    row_tiles, label_tiles = shortlist.shape
    blocks = active.reshape(row_tiles, TILE, label_tiles, TILE) * shortlist[:, None, :, None]
    return blocks.reshape(active.shape).astype(jnp.bfloat16)


def shards(features, direction, active, shortlist):
    vectors = direction[0]
    gathered = lax.all_gather(vectors, "blk", axis=0, tiled=True)
    weights = active_weights(active, shortlist)
    slab_part = lax.all_gather(features, "lab", axis=0, tiled=True)
    margins = lax.dot_general(
        slab_part, gathered, (((1,), (1,)), ((), ())), preferred_element_type=jnp.float32
    )
    scaled = (weights.astype(jnp.float32) * margins).astype(jnp.bfloat16)
    label_sums = lax.dot_general(
        scaled, slab_part, (((0,), (0,)), ((), ())), preferred_element_type=jnp.float32
    )
    own_total = lax.psum_scatter(label_sums, "blk", scatter_dimension=0, tiled=True)
    product = vectors.astype(jnp.float32) + own_total
    curve = jnp.sum(vectors.astype(jnp.float32) * product, axis=-1) / D
    return (product[None], curve[None])


def solution(mesh):
    return jax.shard_map(
        shards,
        mesh=mesh,
        in_specs=(P(("blk", "lab"), None), P("lab", "blk", None), P("blk", "lab"), P("blk", "lab")),
        out_specs=(P("lab", "blk", None), P("lab", "blk")),
        check_vma=False,
    )
```

profile of v0, /device:TPU:8, one launch (start us, length us, event | category | flops | bytes accessed | tf_op | source)
XLA Modules:
  0.0 245.1 jit_solution(11948266229189764883)
XLA Ops:
  7.2 0.0 all-gather.3.cloned.1.call-start
  7.2 0.7 all-gather.3.cloned.1.call-update
  7.9 0.0 reduce-scatter.2.cloned.1.call-start
  7.9 0.8 copy.6
  8.7 47.3 %all-gather = bf16[1,256,768]{2,1,0:T(8,128)(2,1)S(1)} all-gather(bf16[1,16,768]{2,1,0:T(8,128)(2,1)} %param.5), channel_id=2, replica_groups=mesh['blk'=16,'lab'=32] {'blk'}, dimensions={1}, use_global_device_ids=true | all-gather | bytes 417792 | tf_op jit(solution)/shard_map/all_gather | solution.py:18
  56.0 79.5 %all-gather.3.cloned.1.call-done = bf16[4096,768]{1,0:T(8,128)(2,1)} async-done(((bf16[128,768]{1,0:T(8,128)(2,1)}), bf16[4096,768]{1,0:T(8,128)(2,1)}) %all-gather.3.cloned.1.call-update) | async-done | bytes 6291472 | tf_op jit(solution)/shard_map/all_gather | solution.py:20
  135.5 3.2 %mul.17 = s32[32,128,2,128]{3,2,1,0:T(2,128)} broadcast(s32[32,2]{1,0:T(8,128)S(1)} %copy.6), dimensions={0,2} | broadcast | bytes 4194560 | tf_op jit(solution)/shard_map/mul | solution.py:12
  138.7 0.0 copy-start
  138.7 13.8 %fusion.4 = f32[256,768]{1,0:T(8,128)} fusion(bf16[4096,768]{1,0:T(8,128)(2,1)} %all-gather.3.cloned.1.call-done, s32[4096,256]{1,0:T(8,128)} %param.6, s32[512,8,2,128]{3,2,1,0:T(2,128)} %bitcast.25, bf16[1,256,768]{2,1,0:T(8,128)(2,1)S(1)} %all-gather), kind=kOutput, calls=%fused_computation.5 | convolution fusion | flops 3226468352 | bytes 15859712 | tf_op jit(solution)/shard_map/dot_general | solution.py:25
  152.5 0.0 reduce-scatter.2.cloned.1.call-update
  152.5 83.7 %reduce-scatter.2.cloned.1.call-done = f32[16,768]{1,0:T(8,128)} async-done(((f32[256,768]{1,0:T(8,128)}), f32[16,768]{1,0:T(8,128)}) %reduce-scatter.2.cloned.1.call-update) | async-done | bytes 49168 | tf_op jit(solution)/shard_map/reduce_scatter | solution.py:28
  236.2 0.0 copy-done
  236.2 1.5 fusion.6
  237.7 0.5 multiply_bitcast_fusion
Async XLA Ops:
  7.2 128.4 %all-gather.3.cloned.1.call-start = ((), (), s32[]{:S(2)}) async-start(), calls=%async_computation.1 | async-start | bytes 6488064 | tf_op jit(solution)/shard_map/all_gather | solution.py:20
  7.9 228.3 %reduce-scatter.2.cloned.1.call-start = ((), (), s32[]{:S(2)}) async-start(), calls=%async_computation.2 | async-start | bytes 835584 | tf_op jit(solution)/shard_map/reduce_scatter | solution.py:28
  138.7 97.5 %copy-start = (bf16[1,16,768]{2,1,0:T(8,128)(2,1)S(1)}, bf16[1,16,768]{2,1,0:T(8,128)(2,1)}, u32[]{:S(2)}) copy-start(bf16[1,16,768]{2,1,0:T(8,128)(2,1)} %param.5) | copy-start | bytes 73732
Sparse Core Ops, SparseCore 0:
  11.3 124.2 all-gather.2
  152.6 83.4 reduce-scatter.1
where the time goes:
time: 245 us
  waiting for transfers between devices  164 us (67%)
  blocking collectives  47.3 us (19%)
  between operations  14 us (6%)
  matrix products  13.8 us (6%)
  local copies, waits for them, and re-layouts  3.93 us (2%)
    reduce_scatter x1, waiting for transfers between devices, shards(): lax.psum_scatter(label_sums, 'blk', scatter_dimension=0, tiled=True)  83.7 us
    all_gather x1, waiting for transfers between devices, shards(): slab_part = lax.all_gather(features, 'lab', axis=0, tiled=True)  79.5 us
    all_gather x1, blocking collectives, shards(): gathered = lax.all_gather(vectors, 'blk', axis=0, tiled=True)  47.3 us
    dot_general x1, matrix products, shards(): lax.dot_general(scaled, slab_part, (((0,), (0,)), ((), ())), preferred_el...  13.8 us
  transfers between devices with their start and end apart: 2, of which 2 were waited for; matrix products, arithmetic and copies ran while one was open for 0% of the time, Pallas kernels for 0%

commit v1 on v0

--- a/solution.py
+++ b/solution.py
@@ -5,6 +5,13 @@
 
 D = 768
 TILE = 128
+
+
+def swapped_in(array, axis, along):
+    size = lax.axis_size(axis)
+    blocks = jnp.stack([array for _ in range(size)])
+    blocks = lax.all_to_all(blocks, axis, split_axis=0, concat_axis=0)
+    return jnp.concatenate(blocks, axis=along)
 
 
 def active_weights(active, shortlist):
@@ -17,7 +24,7 @@
     vectors = direction[0]
     gathered = lax.all_gather(vectors, "blk", axis=0, tiled=True)
     weights = active_weights(active, shortlist)
-    slab_part = lax.all_gather(features, "lab", axis=0, tiled=True)
+    slab_part = swapped_in(features, "lab", 0)
     margins = lax.dot_general(
         slab_part, gathered, (((1,), (1,)), ((), ())), preferred_element_type=jnp.float32
     )

time: 245 us -> 328 us (1.34)
  blocking collectives: 47.3 us -> 184 us
  waiting for transfers between devices: 164 us -> 89.9 us
  starting transfers between devices: 0.08 us -> 16.4 us
  local copies, waits for them, and re-layouts: 3.93 us -> 7.56 us
    all_gather x1, blocking collectives: 47.3 us -> 184 us  [shards(): gathered = lax.all_gather(vectors, 'blk', axis=0, tiled=True)]
    all_gather x1 -> x0, waiting for transfers between devices: 79.5 us -> none  [shards(): slab_part = lax.all_gather(features, 'lab', axis=0, tiled=True)]
    all_to_all x0 -> x1, starting transfers between devices: none -> 16.3 us  [swapped_in(): blocks = lax.all_to_all(blocks, axis, split_axis=0, concat_axis=0)]
    reduce_scatter x1, waiting for transfers between devices: 83.7 us -> 89.9 us  [shards(): lax.psum_scatter(label_sums, 'blk', scatter_dimension=0, tiled=True)]
    another operation x0 -> x1, local copies, waits for them, and re-layouts: none -> 4.3 us  [swapped_in(): blocks = jnp.stack([array for _ in range(size)])]
  transfers between devices with their start and end apart: 2 -> 2, of which waited for: 2 -> 1; matrix products, arithmetic and copies ran while one was open for 0% -> 0% of each run, Pallas kernels for 0% -> 0%
where the time goes in v1:
time: 328 us; the launch traced here: 327 us
  blocking collectives  184 us (56%)
  waiting for transfers between devices  89.9 us (27%)
  starting transfers between devices  16.4 us (5%)
  between operations  14 us (4%)
  matrix products  13.8 us (4%)
  local copies, waits for them, and re-layouts  7.56 us (2%)
    all_gather x1, blocking collectives, shards(): gathered = lax.all_gather(vectors, 'blk', axis=0, tiled=True)  184 us
    reduce_scatter x1, waiting for transfers between devices, shards(): lax.psum_scatter(label_sums, 'blk', scatter_dimension=0, tiled=True)  89.9 us
    all_to_all x1, starting transfers between devices, swapped_in(): blocks = lax.all_to_all(blocks, axis, split_axis=0, concat_axis=0)  16.3 us
    dot_general x1, matrix products, shards(): lax.dot_general(scaled, slab_part, (((0,), (0,)), ((), ())), preferred_el...  13.8 us
  transfers between devices with their start and end apart: 2, of which 1 were waited for; matrix products, arithmetic and copies ran while one was open for 0% of the time, Pallas kernels for 0%

profile of v1, /device:TPU:8, one launch (start us, length us, event | category | flops | bytes accessed | tf_op | source)
XLA Modules:
  0.0 327.4 jit_solution(12608722988592543245)
XLA Ops:
  7.2 4.3 %stack.2 = bf16[32,128,768]{2,1,0:T(8,128)(2,1)} broadcast(bf16[128,768]{1,0:T(8,128)(2,1)} %param.4), dimensions={1,2} | broadcast | bytes 6488064 | tf_op jit(solution)/shard_map/stack | solution.py:12
  11.5 0.0 copy-start.1
  11.5 0.0 copy-start
  11.5 16.3 %all-to-all-start = ((bf16[32,128,768]{2,1,0:T(8,128)(2,1)}), bf16[32,128,768]{2,1,0:T(8,128)(2,1)}, u32[]{:S(2)}, u32[]{:S(2)}) async-start(bf16[32,128,768]{2,1,0:T(8,128)(2,1)} %stack.2), calls=%async_computation | async-start | bytes 12582912 | tf_op jit(solution)/shard_map/all_to_all | solution.py:13
  27.8 0.0 reduce-scatter.2.cloned.1.call-start
  27.9 0.0 copy-done.1
  27.9 0.1 copy.6
  28.0 0.0 copy-done
  28.0 183.7 %all-gather = bf16[1,256,768]{2,1,0:T(8,128)(2,1)S(1)} all-gather(bf16[1,16,768]{2,1,0:T(8,128)(2,1)S(1)} %copy-done), channel_id=2, replica_groups=mesh['blk'=16,'lab'=32] {'blk'}, dimensions={1}, use_global_device_ids=true | all-gather | bytes 417792 | tf_op jit(solution)/shard_map/all_gather | solution.py:25
  211.6 0.0 all-to-all-done
  211.6 3.2 mul.17
  214.8 13.8 %fusion.4 = f32[256,768]{1,0:T(8,128)} fusion(bf16[4096,768]{1,0:T(8,128)(2,1)} %bitcast.1, s32[4096,256]{1,0:T(8,128)} %param.6, s32[512,8,2,128]{3,2,1,0:T(2,128)} %bitcast.26, bf16[1,256,768]{2,1,0:T(8,128)(2,1)S(1)} %all-gather), kind=kOutput, calls=%fused_computation.5 | convolution fusion | flops 3226468352 | bytes 15859712 | tf_op jit(solution)/shard_map/dot_general | solution.py:32
  228.6 0.0 reduce-scatter.2.cloned.1.call-update
  228.6 89.9 %reduce-scatter.2.cloned.1.call-done = f32[16,768]{1,0:T(8,128)} async-done(((f32[256,768]{1,0:T(8,128)}), f32[16,768]{1,0:T(8,128)}) %reduce-scatter.2.cloned.1.call-update) | async-done | bytes 49168 | tf_op jit(solution)/shard_map/reduce_scatter | solution.py:35
  318.5 1.5 fusion.6
  320.0 0.5 multiply_bitcast_fusion
Async XLA Ops:
  11.5 16.4 %copy-start.1 = (s32[32,2]{0,1:T(2,128)S(1)}, s32[32,2]{0,1:T(2,128)}, u32[]{:S(2)}) copy-start(s32[32,2]{0,1:T(2,128)} %param.7) | copy-start | bytes 772
  11.5 16.5 %copy-start = (bf16[1,16,768]{2,1,0:T(8,128)(2,1)S(1)}, bf16[1,16,768]{2,1,0:T(8,128)(2,1)}, u32[]{:S(2)}) copy-start(bf16[1,16,768]{2,1,0:T(8,128)(2,1)} %param.5) | copy-start | bytes 73732
  11.5 200.1 %all-to-all-start = ((bf16[32,128,768]{2,1,0:T(8,128)(2,1)}), bf16[32,128,768]{2,1,0:T(8,128)(2,1)}, u32[]{:S(2)}, u32[]{:S(2)}) async-start(bf16[32,128,768]{2,1,0:T(8,128)(2,1)} %stack.2), calls=%async_computation | async-start | bytes 12582912 | tf_op jit(solution)/shard_map/all_to_all | solution.py:13
  27.8 290.7 %reduce-scatter.2.cloned.1.call-start = ((), (), s32[]{:S(2)}) async-start(), calls=%async_computation.2 | async-start | bytes 835584 | tf_op jit(solution)/shard_map/reduce_scatter | solution.py:35
Sparse Core Ops, SparseCore 0:
  228.7 89.7 reduce-scatter.1
